TPU v7x, 32 devices: a whole 2x2x4 slice. The times are simulated.
32 devices in a mesh: ctx: 8 (over z, y), dp: 4 (over x, core).
Axes of the slice: x: 2, y: 2, z: 4, core: 2. Of those that a mesh axis runs over, the one named last changes fastest.
Arguments:
- tokens: bfloat16 [4, 4096, 768], P('dp', 'ctx'), may hold values from -6 to 6
- cotangent: bfloat16 [4, 4096, 768], P('dp', 'ctx'), may hold values from -6 to 6
- attn_gain: bfloat16 [768], P('dp'), may hold values from 0.099609375 to 1.8984375
- mlp_gain: bfloat16 [768], P('dp'), may hold values from 0.099609375 to 1.8984375
- w_qkv: bfloat16 [768, 2304], P('dp'), may hold values from -0.21875 to 0.21875
- w_out: bfloat16 [768, 768], P('dp'), may hold values from -6 to 6
- w_in: bfloat16 [768, 2304], P('dp'), may hold values from -0.21875 to 0.21875
- w_mlp_out: bfloat16 [1152, 768], P('dp'), may hold values from -0.1875 to 0.1875
- block_offsets: int32 [4, 8], P('dp', 'ctx'), may hold values from 0 to 3584, as said below
Outputs:
- mixed: bfloat16 [4, 4096, 768], P('dp', 'ctx')
- tokens_grad: float32 [4, 4096, 768], P('dp', 'ctx')
- attn_gain_grad: float32 [768], P('dp')
- mlp_gain_grad: float32 [768], P('dp')
- w_qkv_grad: float32 [768, 2304], P('dp')
- w_out_grad: float32 [768, 768], P('dp')
- w_in_grad: float32 [768, 2304], P('dp')
- w_mlp_out_grad: float32 [1152, 768], P('dp')
Inputs may be any that keep to these rules, and one draw needn't show every extreme that they name: `block_offsets`: each row holds every multiple of 512 below 4096 exactly once.
All inputs are finite; a program needn't handle non-finite values.
Results may differ from a plain program's by a relative error of at most 0.022.
Values may be sent and summed in bfloat16 or wider, within the bound.
No kernel may reach another device: no remote copies, remote signals or barrier semaphores. Data moves between devices by JAX's collectives and lax.ppermute only.
A program may use at most 128 MiB of HBM per device.

v0:
```python
import jax
import jax.numpy as jnp
from jax import lax
from jax.sharding import PartitionSpec as P

HEADS = 12
HEAD_DIM = 64
FF = 1152
rope_base = 160000.0
norm_eps = 1e-05


def passed_along(x, axis, by):
    count = lax.axis_size(axis)
    return lax.ppermute(x, axis, [(i, (i + by) % count) for i in range(count)])


def layer_norm(values, gain):
    center = values - jnp.mean(values, axis=-1, keepdims=True)
    spread = jnp.mean(center * center, axis=-1, keepdims=True)
    return center * lax.rsqrt(spread + norm_eps) * gain


def norm_back(values, gain, upstream):
    _, pull = jax.vjp(layer_norm, values, gain)
    return pull(upstream)


def rotary_tables(positions, half_size):
    frequency = rope_base ** (-jnp.arange(half_size, dtype=jnp.float32) / half_size)
    angles = positions[:, None] * frequency[None, :]
    cosine = jnp.cos(angles)
    sine_table = jnp.sin(angles)
    return (jnp.concatenate([cosine, cosine], -1), jnp.concatenate([sine_table, sine_table], -1))


def rotate(values, cosine, sine_table):
    half_size = values.shape[-1] // 2
    turned = jnp.concatenate([-values[..., half_size:], values[..., :half_size]], -1)
    return values * cosine[:, None, :] + turned * sine_table[:, None, :]


def unrotate(upstream, cosine, sine_table):
    half_size = upstream.shape[-1] // 2
    turned = upstream * sine_table[:, None, :]
    return upstream * cosine[:, None, :] + jnp.concatenate(
        [turned[..., half_size:], -turned[..., :half_size]], -1
    )


def geglu(packed, hidden_size):
    return jax.nn.gelu(packed[:, :hidden_size], approximate=False) * packed[:, hidden_size:]


def product(left, right):
    return jnp.dot(left, right, preferred_element_type=jnp.float32)


def transposed_left(left, right):
    return lax.dot_general(
        left, right, (((0,), (0,)), ((), ())), preferred_element_type=jnp.float32
    )


def transposed_right(left, right):
    return lax.dot_general(
        left, right, (((1,), (1,)), ((), ())), preferred_element_type=jnp.float32
    )


def key_block():
    return 512


def body(tokens, cotangent, attn_gain, mlp_gain, w_qkv, w_out, w_in, w_mlp_out, block_offsets):
    head_count = HEADS
    head_size = HEAD_DIM
    hidden_size = FF
    model_width = head_count * head_size
    scale = head_size ** (-0.5)
    inputs = tokens[0].astype(jnp.float32)
    row_count = inputs.shape[0]
    positions = (block_offsets[0, 0] + jnp.arange(row_count, dtype=jnp.int32)).astype(jnp.float32)
    cosine, sine_table = rotary_tables(positions, head_size // 2)
    gain_one, gain_two, weight_qkv, weight_out, weight_in, weight_down = (
        lax.all_gather(attn_gain, "dp", axis=0, tiled=True),
        lax.all_gather(mlp_gain, "dp", axis=0, tiled=True),
        lax.all_gather(w_qkv, "dp", axis=0, tiled=True),
        lax.all_gather(w_out, "dp", axis=0, tiled=True),
        lax.all_gather(w_in, "dp", axis=0, tiled=True),
        lax.all_gather(w_mlp_out, "dp", axis=0, tiled=True),
    )
    first_gain = gain_one.astype(jnp.float32)
    second_gain = gain_two.astype(jnp.float32)
    normed = layer_norm(inputs, first_gain).astype(jnp.bfloat16)
    packed = product(normed, weight_qkv).reshape(row_count, 3, head_count, head_size)
    queries = rotate(packed[:, 0], cosine, sine_table).astype(jnp.bfloat16)
    keys_local = (
        rotate(packed[:, 1], cosine, sine_table)
        .astype(jnp.bfloat16)
        .reshape(row_count, model_width)
    )
    values_local = packed[:, 2].astype(jnp.bfloat16).reshape(row_count, model_width)

    def attend(carried, blocks):
        running_max, running_sum, running_out = carried
        key_part, value_part = blocks
        scores = (
            jnp.einsum("qhd,khd->hqk", queries, key_part, preferred_element_type=jnp.float32)
            * scale
        )
        new_max = jnp.maximum(running_max, jnp.max(scores, axis=-1))
        rescale = jnp.exp(running_max - new_max)
        weights = jnp.exp(scores - new_max[:, :, None])
        running_sum = running_sum * rescale + jnp.sum(weights, axis=-1)
        running_out = running_out * rescale.T[:, :, None] + jnp.einsum(
            "hqk,khd->qhd",
            weights.astype(jnp.bfloat16),
            value_part,
            preferred_element_type=jnp.float32,
        )
        return ((new_max, running_sum, running_out), None)

    initial = (
        jnp.full((head_count, row_count), -1e30, jnp.float32),
        jnp.zeros((head_count, row_count), jnp.float32),
        jnp.zeros((row_count, head_count, head_size), jnp.float32),
    )
    carried = initial
    shards = (
        lax.all_gather(keys_local, "ctx", axis=0, tiled=True),
        lax.all_gather(values_local, "ctx", axis=0, tiled=True),
    )
    key_count = shards[0].shape[0]
    block_size = key_block()
    split_keys = shards[0].reshape(key_count // block_size, block_size, head_count, head_size)
    split_values = shards[1].reshape(key_count // block_size, block_size, head_count, head_size)
    carried, _ = lax.scan(attend, carried, (split_keys, split_values))
    running_max, running_sum, running_out = carried
    attended = running_out / running_sum.T[:, :, None]
    log_total = running_max + jnp.log(running_sum)
    attended_low = attended.reshape(row_count, model_width).astype(jnp.bfloat16)
    residual = inputs + product(attended_low, weight_out)
    mlp_normed = layer_norm(residual, second_gain).astype(jnp.bfloat16)
    up_gate = product(mlp_normed, weight_in)
    joined = geglu(up_gate, hidden_size).astype(jnp.bfloat16)
    outputs = residual + product(joined, weight_down)
    mixed = outputs.astype(jnp.bfloat16)[None]
    gain_one, gain_two, weight_qkv, weight_out, weight_in, weight_down = (
        lax.all_gather(attn_gain, "dp", axis=0, tiled=True),
        lax.all_gather(mlp_gain, "dp", axis=0, tiled=True),
        lax.all_gather(w_qkv, "dp", axis=0, tiled=True),
        lax.all_gather(w_out, "dp", axis=0, tiled=True),
        lax.all_gather(w_in, "dp", axis=0, tiled=True),
        lax.all_gather(w_mlp_out, "dp", axis=0, tiled=True),
    )
    first_gain = gain_one.astype(jnp.float32)
    second_gain = gain_two.astype(jnp.float32)
    upstream = cotangent[0].astype(jnp.float32)
    upstream_low = upstream.astype(jnp.bfloat16)
    grad_down = transposed_left(joined, upstream_low)
    grad_joined = transposed_right(upstream_low, weight_down)
    _, glu_pull = jax.vjp(lambda packed_in: geglu(packed_in, hidden_size), up_gate)
    grad_up_gate = glu_pull(grad_joined)[0].astype(jnp.bfloat16)
    grad_in = transposed_left(mlp_normed, grad_up_gate)
    grad_mlp_normed = transposed_right(grad_up_gate, weight_in)
    grad_residual_norm, grad_gain_two = norm_back(residual, second_gain, grad_mlp_normed)
    grad_residual = upstream + grad_residual_norm
    residual_low = grad_residual.astype(jnp.bfloat16)
    grad_out = transposed_left(attended_low, residual_low)
    grad_attended = (
        transposed_right(residual_low, weight_out)
        .astype(jnp.bfloat16)
        .reshape(row_count, head_count, head_size)
    )
    row_delta = jnp.sum(grad_attended.astype(jnp.float32) * attended, axis=-1).T

    def block_grads(query_rows, grad_rows, log_rows, delta_rows, key_rows, value_rows):
        key_count = key_rows.shape[0]
        query_count = query_rows.shape[0]
        block_size = key_block()
        split_keys = key_rows.reshape(key_count // block_size, block_size, head_count, head_size)
        split_values = value_rows.reshape(
            key_count // block_size, block_size, head_count, head_size
        )

        def backward_block(query_grad, blocks):
            key_part, value_part = blocks
            scores = (
                jnp.einsum("qhd,khd->hqk", query_rows, key_part, preferred_element_type=jnp.float32)
                * scale
            )
            probs = jnp.exp(scores - log_rows[:, :, None])
            prob_grad = jnp.einsum(
                "qhd,khd->hqk", grad_rows, value_part, preferred_element_type=jnp.float32
            )
            score_grad = (probs * (prob_grad - delta_rows[:, :, None])).astype(jnp.bfloat16)
            value_grad = jnp.einsum(
                "hqk,qhd->khd",
                probs.astype(jnp.bfloat16),
                grad_rows,
                preferred_element_type=jnp.float32,
            )
            key_grad = (
                jnp.einsum(
                    "hqk,qhd->khd", score_grad, query_rows, preferred_element_type=jnp.float32
                )
                * scale
            )
            query_grad = (
                query_grad
                + jnp.einsum(
                    "hqk,khd->qhd", score_grad, key_part, preferred_element_type=jnp.float32
                )
                * scale
            )
            return (
                query_grad,
                (
                    key_grad.reshape(block_size, model_width),
                    value_grad.reshape(block_size, model_width),
                ),
            )

        query_start = jnp.zeros((query_count, head_count, head_size), jnp.float32)
        query_grad, (key_grad, value_grad) = lax.scan(
            backward_block, query_start, (split_keys, split_values)
        )
        return (
            query_grad,
            key_grad.reshape(key_count, model_width),
            value_grad.reshape(key_count, model_width),
        )

    zero_rows = jnp.zeros((row_count, model_width), jnp.float32)
    zero_heads = jnp.zeros((row_count, head_count, head_size), jnp.float32)

    def cycle_turn(turn_index, carried):
        key_rows, value_rows, key_sum, value_sum, query_sum = carried
        query_add, key_add, value_add = block_grads(
            queries, grad_attended, log_total, row_delta, key_rows, value_rows
        )
        key_sum = key_sum + key_add
        value_sum = value_sum + value_add
        key_rows, value_rows = passed_along((key_rows, value_rows), "ctx", 1)
        key_sum, value_sum = (
            passed_along(key_sum.astype(jnp.bfloat16), "ctx", 1).astype(key_sum.dtype),
            passed_along(value_sum.astype(jnp.bfloat16), "ctx", 1).astype(value_sum.dtype),
        )
        return (key_rows, value_rows, key_sum, value_sum, query_sum + query_add)

    start_state = (keys_local, values_local, zero_rows, zero_rows, zero_heads)
    _, _, grad_keys, grad_values, grad_queries = lax.fori_loop(
        0, lax.axis_size("ctx"), cycle_turn, start_state
    )
    query_back = unrotate(grad_queries, cosine, sine_table).reshape(row_count, model_width)
    key_back = unrotate(
        grad_keys.reshape(row_count, head_count, head_size), cosine, sine_table
    ).reshape(row_count, model_width)
    grad_packed = jnp.concatenate([query_back, key_back, grad_values], axis=1).astype(jnp.bfloat16)
    grad_qkv = transposed_left(normed, grad_packed)
    grad_normed = transposed_right(grad_packed, weight_qkv)
    grad_inputs_norm, grad_gain_one = norm_back(inputs, first_gain, grad_normed)
    tokens_grad = (grad_residual + grad_inputs_norm)[None]
    summed = (
        lax.psum_scatter(
            grad_gain_one.astype(jnp.bfloat16), "dp", scatter_dimension=0, tiled=True
        ).astype(jnp.float32),
        lax.psum_scatter(
            grad_gain_two.astype(jnp.bfloat16), "dp", scatter_dimension=0, tiled=True
        ).astype(jnp.float32),
        lax.psum_scatter(
            grad_qkv.astype(jnp.bfloat16), "dp", scatter_dimension=0, tiled=True
        ).astype(jnp.float32),
        lax.psum_scatter(
            grad_out.astype(jnp.bfloat16), "dp", scatter_dimension=0, tiled=True
        ).astype(jnp.float32),
        lax.psum_scatter(
            grad_in.astype(jnp.bfloat16), "dp", scatter_dimension=0, tiled=True
        ).astype(jnp.float32),
        lax.psum_scatter(
            grad_down.astype(jnp.bfloat16), "dp", scatter_dimension=0, tiled=True
        ).astype(jnp.float32),
    )
    totals = (
        lax.psum(summed[0].astype(jnp.bfloat16), "ctx").astype(jnp.float32),
        lax.psum(summed[1].astype(jnp.bfloat16), "ctx").astype(jnp.float32),
        lax.psum(summed[2].astype(jnp.bfloat16), "ctx").astype(jnp.float32),
        lax.psum(summed[3].astype(jnp.bfloat16), "ctx").astype(jnp.float32),
        lax.psum(summed[4].astype(jnp.bfloat16), "ctx").astype(jnp.float32),
        lax.psum(summed[5].astype(jnp.bfloat16), "ctx").astype(jnp.float32),
    )
    return (mixed, tokens_grad, totals[0], totals[1], totals[2], totals[3], totals[4], totals[5])


def solution(mesh):
    return jax.shard_map(
        body,
        mesh=mesh,
        in_specs=(
            P("dp", "ctx", None),
            P("dp", "ctx", None),
            P("dp"),
            P("dp"),
            P("dp", None),
            P("dp", None),
            P("dp", None),
            P("dp", None),
            P("dp", "ctx"),
        ),
        out_specs=(
            P("dp", "ctx", None),
            P("dp", "ctx", None),
            P("dp"),
            P("dp"),
            P("dp", None),
            P("dp", None),
            P("dp", None),
            P("dp", None),
        ),
        check_vma=False,
    )
```

profile of v0, /device:TPU:0, one launch (start us, length us, event | category | flops | bytes accessed | tf_op | source)
XLA Modules:
  0.0 1304.9 jit_solution(13983983818318694424)
XLA Ops:
  21.6 21.4 %all-gather.7.cloned.1.call-done = bf16[768,2304]{1,0:T(8,128)(2,1)} async-done(((bf16[192,2304]{1,0:T(8,128)(2,1)}), bf16[768,2304]{1,0:T(8,128)(2,1)}) %all-gather.7.cloned.1.call-update) | async-done | bytes 3538960 | tf_op jit(solution)/shard_map/all_gather | solution.py:88
  61.9 95.1 %all-gather.9.cloned.1.call-done = bf16[4096,768]{0,1:T(8,128)(2,1)} async-done(((bf16[512,768]{0,1:T(8,128)(2,1)}), bf16[4096,768]{0,1:T(8,128)(2,1)}) %all-gather.9.cloned.1.call-update) | async-done | bytes 6291472 | tf_op jit(solution)/shard_map/all_gather | solution.py:131
  168.8 87.9 %all-gather.11.cloned.1.call-done = bf16[4096,768]{0,1:T(8,128)(2,1)} async-done(((bf16[512,768]{0,1:T(8,128)(2,1)}), bf16[4096,768]{0,1:T(8,128)(2,1)}) %all-gather.11.cloned.1.call-update) | async-done | bytes 6291472 | tf_op jit(solution)/shard_map/all_gather | solution.py:132
  268.8 145.5 %while.40 = (s32[]{:T(128)}, f32[12,512]{1,0:T(8,128)S(1)}, f32[12,512]{1,0:T(8,128)S(1)}, f32[512,12,64]{0,2,1:T(8,128)S(1)}, bf16[8,512,12,64]{1,3,2,0:T(8,128...) while((s32[]{:T(128)}, f32[12,512]{1,0:T(8,128)S(1)}, ...), condition=%wide.region_5.6_spmd.clone, body=%wide.region_2.5_spmd.clone.sunk | while | flops 831688704 | bytes 93979776 | solution.py:138
  461.1 664.6 %while.41 = (s32[]{:T(128)}, bf16[512,768]{0,1:T(8,128)(2,1)}, bf16[512,768]{0,1:T(8,128)(2,1)}, f32[512,768]{0,1:T(8,128)}, f32[512,768]{0,1:T(8,128)}, /*index...) while((s32[]{:T(128)}, bf16[512,768]{0,1:T(8,128)(2,1)}, ...), condition=%wide.region_12.13_spmd.clone, body=%wide.region_11.12_spmd.clone.sunk | while | flops 2043150336 | bytes 191177200 | solution.py:253
  498.8 15.6 %collective-permute-done.3 = bf16[512,768]{0,1:T(8,128)(2,1)} collective-permute-done((bf16[512,768]{0,1:T(8,128)(2,1)}, bf16[512,768]{0,1:T(8,128)(2,1)}, u32[]{:S(2)}, u32[]{:S(2)}) %collective-permute-start.3) | collective-permute-done | bytes 786464 | tf_op jit(solution)/shard_map/while/body/eval_jaxpr/ppermute | solution.py:15
  516.9 14.3 %collective-permute-done = bf16[512,768]{0,1:T(8,128)(2,1)} collective-permute-done((bf16[512,768]{0,1:T(8,128)(2,1)S(1)}, bf16[512,768]{0,1:T(8,128)(2,1)}, u32[]{:S(2)}, u32[]{:S(2)}) %collective-permute-start) | collective-permute-done | bytes 786464 | tf_op jit(solution)/shard_map/while/body/eval_jaxpr/ppermute | solution.py:15
  531.2 14.9 %collective-permute-done.1 = bf16[512,768]{0,1:T(8,128)(2,1)} collective-permute-done((bf16[512,768]{0,1:T(8,128)(2,1)S(1)}, bf16[512,768]{0,1:T(8,128)(2,1)}, u32[]{:S(2)}, u32[]{:S(2)}) %collective-permute-start.1) | collective-permute-done | bytes 786464 | tf_op jit(solution)/shard_map/while/body/eval_jaxpr/ppermute | solution.py:15
  585.0 15.6 %collective-permute-done.3 = bf16[512,768]{0,1:T(8,128)(2,1)} collective-permute-done((bf16[512,768]{0,1:T(8,128)(2,1)}, bf16[512,768]{0,1:T(8,128)(2,1)}, u32[]{:S(2)}, u32[]{:S(2)}) %collective-permute-start.3) | collective-permute-done | bytes 786464 | tf_op jit(solution)/shard_map/while/body/eval_jaxpr/ppermute | solution.py:15
  603.1 14.4 %collective-permute-done = bf16[512,768]{0,1:T(8,128)(2,1)} collective-permute-done((bf16[512,768]{0,1:T(8,128)(2,1)S(1)}, bf16[512,768]{0,1:T(8,128)(2,1)}, u32[]{:S(2)}, u32[]{:S(2)}) %collective-permute-start) | collective-permute-done | bytes 786464 | tf_op jit(solution)/shard_map/while/body/eval_jaxpr/ppermute | solution.py:15
  617.4 14.0 %collective-permute-done.1 = bf16[512,768]{0,1:T(8,128)(2,1)} collective-permute-done((bf16[512,768]{0,1:T(8,128)(2,1)S(1)}, bf16[512,768]{0,1:T(8,128)(2,1)}, u32[]{:S(2)}, u32[]{:S(2)}) %collective-permute-start.1) | collective-permute-done | bytes 786464 | tf_op jit(solution)/shard_map/while/body/eval_jaxpr/ppermute | solution.py:15
  670.3 15.6 %collective-permute-done.3 = bf16[512,768]{0,1:T(8,128)(2,1)} collective-permute-done((bf16[512,768]{0,1:T(8,128)(2,1)}, bf16[512,768]{0,1:T(8,128)(2,1)}, u32[]{:S(2)}, u32[]{:S(2)}) %collective-permute-start.3) | collective-permute-done | bytes 786464 | tf_op jit(solution)/shard_map/while/body/eval_jaxpr/ppermute | solution.py:15
  688.4 14.4 %collective-permute-done = bf16[512,768]{0,1:T(8,128)(2,1)} collective-permute-done((bf16[512,768]{0,1:T(8,128)(2,1)S(1)}, bf16[512,768]{0,1:T(8,128)(2,1)}, u32[]{:S(2)}, u32[]{:S(2)}) %collective-permute-start) | collective-permute-done | bytes 786464 | tf_op jit(solution)/shard_map/while/body/eval_jaxpr/ppermute | solution.py:15
  702.8 13.1 %collective-permute-done.1 = bf16[512,768]{0,1:T(8,128)(2,1)} collective-permute-done((bf16[512,768]{0,1:T(8,128)(2,1)S(1)}, bf16[512,768]{0,1:T(8,128)(2,1)}, u32[]{:S(2)}, u32[]{:S(2)}) %collective-permute-start.1) | collective-permute-done | bytes 786464 | tf_op jit(solution)/shard_map/while/body/eval_jaxpr/ppermute | solution.py:15
  754.9 15.6 %collective-permute-done.3 = bf16[512,768]{0,1:T(8,128)(2,1)} collective-permute-done((bf16[512,768]{0,1:T(8,128)(2,1)}, bf16[512,768]{0,1:T(8,128)(2,1)}, u32[]{:S(2)}, u32[]{:S(2)}) %collective-permute-start.3) | collective-permute-done | bytes 786464 | tf_op jit(solution)/shard_map/while/body/eval_jaxpr/ppermute | solution.py:15
  772.9 14.4 %collective-permute-done = bf16[512,768]{0,1:T(8,128)(2,1)} collective-permute-done((bf16[512,768]{0,1:T(8,128)(2,1)S(1)}, bf16[512,768]{0,1:T(8,128)(2,1)}, u32[]{:S(2)}, u32[]{:S(2)}) %collective-permute-start) | collective-permute-done | bytes 786464 | tf_op jit(solution)/shard_map/while/body/eval_jaxpr/ppermute | solution.py:15
  787.3 12.3 collective-permute-done.1
  838.5 15.6 %collective-permute-done.3 = bf16[512,768]{0,1:T(8,128)(2,1)} collective-permute-done((bf16[512,768]{0,1:T(8,128)(2,1)}, bf16[512,768]{0,1:T(8,128)(2,1)}, u32[]{:S(2)}, u32[]{:S(2)}) %collective-permute-start.3) | collective-permute-done | bytes 786464 | tf_op jit(solution)/shard_map/while/body/eval_jaxpr/ppermute | solution.py:15
  856.6 14.4 %collective-permute-done = bf16[512,768]{0,1:T(8,128)(2,1)} collective-permute-done((bf16[512,768]{0,1:T(8,128)(2,1)S(1)}, bf16[512,768]{0,1:T(8,128)(2,1)}, u32[]{:S(2)}, u32[]{:S(2)}) %collective-permute-start) | collective-permute-done | bytes 786464 | tf_op jit(solution)/shard_map/while/body/eval_jaxpr/ppermute | solution.py:15
  871.0 11.4 collective-permute-done.1
  910.6 9.3 collective-permute-done.2
  921.3 15.6 %collective-permute-done.3 = bf16[512,768]{0,1:T(8,128)(2,1)} collective-permute-done((bf16[512,768]{0,1:T(8,128)(2,1)}, bf16[512,768]{0,1:T(8,128)(2,1)}, u32[]{:S(2)}, u32[]{:S(2)}) %collective-permute-start.3) | collective-permute-done | bytes 786464 | tf_op jit(solution)/shard_map/while/body/eval_jaxpr/ppermute | solution.py:15
  939.4 14.4 %collective-permute-done = bf16[512,768]{0,1:T(8,128)(2,1)} collective-permute-done((bf16[512,768]{0,1:T(8,128)(2,1)S(1)}, bf16[512,768]{0,1:T(8,128)(2,1)}, u32[]{:S(2)}, u32[]{:S(2)}) %collective-permute-start) | collective-permute-done | bytes 786464 | tf_op jit(solution)/shard_map/while/body/eval_jaxpr/ppermute | solution.py:15
  953.8 10.6 collective-permute-done.1
  1003.2 15.6 %collective-permute-done.3 = bf16[512,768]{0,1:T(8,128)(2,1)} collective-permute-done((bf16[512,768]{0,1:T(8,128)(2,1)}, bf16[512,768]{0,1:T(8,128)(2,1)}, u32[]{:S(2)}, u32[]{:S(2)}) %collective-permute-start.3) | collective-permute-done | bytes 786464 | tf_op jit(solution)/shard_map/while/body/eval_jaxpr/ppermute | solution.py:15
  1021.3 14.4 %collective-permute-done = bf16[512,768]{0,1:T(8,128)(2,1)} collective-permute-done((bf16[512,768]{0,1:T(8,128)(2,1)S(1)}, bf16[512,768]{0,1:T(8,128)(2,1)}, u32[]{:S(2)}, u32[]{:S(2)}) %collective-permute-start) | collective-permute-done | bytes 786464 | tf_op jit(solution)/shard_map/while/body/eval_jaxpr/ppermute | solution.py:15
  1035.7 9.7 collective-permute-done.1
  1084.3 15.6 %collective-permute-done.3 = bf16[512,768]{0,1:T(8,128)(2,1)} collective-permute-done((bf16[512,768]{0,1:T(8,128)(2,1)}, bf16[512,768]{0,1:T(8,128)(2,1)}, u32[]{:S(2)}, u32[]{:S(2)}) %collective-permute-start.3) | collective-permute-done | bytes 786464 | tf_op jit(solution)/shard_map/while/body/eval_jaxpr/ppermute | solution.py:15
  1102.4 14.4 %collective-permute-done = bf16[512,768]{0,1:T(8,128)(2,1)} collective-permute-done((bf16[512,768]{0,1:T(8,128)(2,1)S(1)}, bf16[512,768]{0,1:T(8,128)(2,1)}, u32[]{:S(2)}, u32[]{:S(2)}) %collective-permute-start) | collective-permute-done | bytes 786464 | tf_op jit(solution)/shard_map/while/body/eval_jaxpr/ppermute | solution.py:15
  1138.0 37.4 %reduce-scatter.5.cloned.1.call-done = bf16[192,2304]{1,0:T(8,128)(2,1)} async-done(((bf16[768,2304]{1,0:T(8,128)(2,1)}), bf16[192,2304]{1,0:T(8,128)(2,1)}) %reduce-scatter.5.cloned.1.call-update) | async-done | bytes 884752 | tf_op jit(solution)/shard_map/reduce_scatter | solution.py:272
  1188.3 22.7 %all-reduce.6 = (bf16[192]{0:T(256)(128)(2,1)S(1)}, bf16[192]{0:T(256)(128)(2,1)S(1)}) all-reduce(bf16[192]{0:T(256)(128)(2,1)S(1)} %dynamic-slice.3, bf16[192]{0:T(256)(128)(2,1)S(1)} %dynamic-slice.5), channel_id=1, replica_groups=mesh['ctx'=8,'dp'=4] {'ctx'}, use_global_device_ids=true, to_apply=%region_17.18 | all-reduce | flops 384 | bytes 1536 | tf_op jit(solution)/shard_map/psum | solution.py:286
  1217.6 74.8 %all-reduce.12.cloned.1.call-done = (bf16[192,2304]{1,0:T(8,128)(2,1)}, bf16[192,768]{1,0:T(8,128)(2,1)}, bf16[192,2304]{1,0:T(8,128)(2,1)}, bf16[288,768]{1,0:T(8,128)(2,1)}) async-done(((bf16[192,2304]{1,0:T(8,128)(2,1)}, bf16[192,768]{1,0:T(8,128)(2,1)}, bf16[192,2304]{1,0:T(8,128)(2,1)}, bf16[288,768]{1,0:T(8,128)(2,1)}), (bf16[192,2304]{1,0:T(8,128)(2,1)}, bf16[192,768]{1,0:T(8,128)(2,1)}, ...) | async-done | bytes 2506768 | tf_op jit(solution)/shard_map/psum | solution.py:288
  (497 shorter events, 612.6 us)
Async XLA Ops:
  7.2 35.9 %all-gather.7.cloned.1.call-start = ((), (), s32[]{:S(2)}) async-start(), calls=%async_computation.4 | async-start | bytes 4423680 | tf_op jit(solution)/shard_map/all_gather | solution.py:88
  7.9 149.1 %all-gather.9.cloned.1.call-start = ((), (), s32[]{:S(2)}) async-start(), calls=%async_computation.5 | async-start | bytes 7077888 | tf_op jit(solution)/shard_map/all_gather | solution.py:131
  57.3 199.4 %all-gather.11.cloned.1.call-start = ((), (), s32[]{:S(2)}) async-start(), calls=%async_computation.6 | async-start | bytes 7077888 | tf_op jit(solution)/shard_map/all_gather | solution.py:132
  59.9 355.8 %all-gather.13.cloned.1.call-start = ((), (), s32[]{:S(2)}) async-start(), calls=%async_computation.7 | async-start | bytes 1474560 | tf_op jit(solution)/shard_map/all_gather | solution.py:89
  60.5 359.1 %all-gather.15.cloned.1.call-start = ((), (), s32[]{:S(2)}) async-start(), calls=%async_computation.8 | async-start | bytes 4423680 | tf_op jit(solution)/shard_map/all_gather | solution.py:90
  61.1 365.4 %all-gather.17.cloned.1.call-start = ((), (), s32[]{:S(2)}) async-start(), calls=%async_computation.9 | async-start | bytes 2211840 | tf_op jit(solution)/shard_map/all_gather | solution.py:91
  61.6 1076.3 %reduce-scatter.7.cloned.1.call-start = ((), (), s32[]{:S(2)}) async-start(), calls=%async_computation.11 | async-start | bytes 1474560 | tf_op jit(solution)/shard_map/reduce_scatter | solution.py:275
  446.7 691.2 %reduce-scatter.11.cloned.1.call-start = ((), (), s32[]{:S(2)}) async-start(), calls=%async_computation.13 | async-start | bytes 2211840 | tf_op jit(solution)/shard_map/reduce_scatter | solution.py:281
  449.1 688.9 %reduce-scatter.9.cloned.1.call-start = ((), (), s32[]{:S(2)}) async-start(), calls=%async_computation.12 | async-start | bytes 4423680 | tf_op jit(solution)/shard_map/reduce_scatter | solution.py:278
  461.0 714.4 %reduce-scatter.5.cloned.1.call-start = ((), (), s32[]{:S(2)}) async-start(), calls=%async_computation.10 | async-start | bytes 4423680 | tf_op jit(solution)/shard_map/reduce_scatter | solution.py:272
  483.4 47.8 %collective-permute-start = (bf16[512,768]{0,1:T(8,128)(2,1)S(1)}, bf16[512,768]{0,1:T(8,128)(2,1)}, u32[]{:S(2)}, u32[]{:S(2)}) collective-permute-start(bf16[512,768]{0,1:T(8,128)(2,1)S(1)} %copy.58), channel_id=1, source_target_pairs={{0,4},{4,8},{8,12},{12,16},{16,20},{20,24},{24,28},{28,0},{1,5},{5... | collective-permute-start | bytes 2359304 | tf_op jit(solution)/shard_map/while/body/eval_jaxpr/ppermute | solution.py:15
  483.4 62.7 %collective-permute-start.1 = (bf16[512,768]{0,1:T(8,128)(2,1)S(1)}, bf16[512,768]{0,1:T(8,128)(2,1)}, u32[]{:S(2)}, u32[]{:S(2)}) collective-permute-start(bf16[512,768]{0,1:T(8,128)(2,1)S(1)} %copy-done.6), channel_id=1, source_target_pairs={{0,4},{4,8},{8,12},{12,16},{16,20},{20,24},{24,28},{28,0},{1,5},{5... | collective-permute-start | bytes 2359304 | tf_op jit(solution)/shard_map/while/body/eval_jaxpr/ppermute | solution.py:15
  567.8 32.7 %collective-permute-start.3 = (bf16[512,768]{0,1:T(8,128)(2,1)}, bf16[512,768]{0,1:T(8,128)(2,1)}, u32[]{:S(2)}, u32[]{:S(2)}) collective-permute-start(bf16[512,768]{0,1:T(8,128)(2,1)} %fusion.153), channel_id=1, source_target_pairs={{0,4},{4,8},{8,12},{12,16},{16,20},{20,24},{24,28},{28,0},{1,5},{5... | collective-permute-start | bytes 2359304 | tf_op jit(solution)/shard_map/while/body/eval_jaxpr/ppermute | solution.py:15
  568.8 48.6 %collective-permute-start = (bf16[512,768]{0,1:T(8,128)(2,1)S(1)}, bf16[512,768]{0,1:T(8,128)(2,1)}, u32[]{:S(2)}, u32[]{:S(2)}) collective-permute-start(bf16[512,768]{0,1:T(8,128)(2,1)S(1)} %copy.58), channel_id=1, source_target_pairs={{0,4},{4,8},{8,12},{12,16},{16,20},{20,24},{24,28},{28,0},{1,5},{5... | collective-permute-start | bytes 2359304 | tf_op jit(solution)/shard_map/while/body/eval_jaxpr/ppermute | solution.py:15
  568.9 62.5 %collective-permute-start.1 = (bf16[512,768]{0,1:T(8,128)(2,1)S(1)}, bf16[512,768]{0,1:T(8,128)(2,1)}, u32[]{:S(2)}, u32[]{:S(2)}) collective-permute-start(bf16[512,768]{0,1:T(8,128)(2,1)S(1)} %copy-done.6), channel_id=1, source_target_pairs={{0,4},{4,8},{8,12},{12,16},{16,20},{20,24},{24,28},{28,0},{1,5},{5... | collective-permute-start | bytes 2359304 | tf_op jit(solution)/shard_map/while/body/eval_jaxpr/ppermute | solution.py:15
  653.7 49.1 %collective-permute-start = (bf16[512,768]{0,1:T(8,128)(2,1)S(1)}, bf16[512,768]{0,1:T(8,128)(2,1)}, u32[]{:S(2)}, u32[]{:S(2)}) collective-permute-start(bf16[512,768]{0,1:T(8,128)(2,1)S(1)} %copy.58), channel_id=1, source_target_pairs={{0,4},{4,8},{8,12},{12,16},{16,20},{20,24},{24,28},{28,0},{1,5},{5... | collective-permute-start | bytes 2359304 | tf_op jit(solution)/shard_map/while/body/eval_jaxpr/ppermute | solution.py:15
  653.8 62.1 %collective-permute-start.1 = (bf16[512,768]{0,1:T(8,128)(2,1)S(1)}, bf16[512,768]{0,1:T(8,128)(2,1)}, u32[]{:S(2)}, u32[]{:S(2)}) collective-permute-start(bf16[512,768]{0,1:T(8,128)(2,1)S(1)} %copy-done.6), channel_id=1, source_target_pairs={{0,4},{4,8},{8,12},{12,16},{16,20},{20,24},{24,28},{28,0},{1,5},{5... | collective-permute-start | bytes 2359304 | tf_op jit(solution)/shard_map/while/body/eval_jaxpr/ppermute | solution.py:15
  737.7 32.7 %collective-permute-start.3 = (bf16[512,768]{0,1:T(8,128)(2,1)}, bf16[512,768]{0,1:T(8,128)(2,1)}, u32[]{:S(2)}, u32[]{:S(2)}) collective-permute-start(bf16[512,768]{0,1:T(8,128)(2,1)} %fusion.153), channel_id=1, source_target_pairs={{0,4},{4,8},{8,12},{12,16},{16,20},{20,24},{24,28},{28,0},{1,5},{5... | collective-permute-start | bytes 2359304 | tf_op jit(solution)/shard_map/while/body/eval_jaxpr/ppermute | solution.py:15
  737.8 49.5 %collective-permute-start = (bf16[512,768]{0,1:T(8,128)(2,1)S(1)}, bf16[512,768]{0,1:T(8,128)(2,1)}, u32[]{:S(2)}, u32[]{:S(2)}) collective-permute-start(bf16[512,768]{0,1:T(8,128)(2,1)S(1)} %copy.58), channel_id=1, source_target_pairs={{0,4},{4,8},{8,12},{12,16},{16,20},{20,24},{24,28},{28,0},{1,5},{5... | collective-permute-start | bytes 2359304 | tf_op jit(solution)/shard_map/while/body/eval_jaxpr/ppermute | solution.py:15
  737.9 61.7 %collective-permute-start.1 = (bf16[512,768]{0,1:T(8,128)(2,1)S(1)}, bf16[512,768]{0,1:T(8,128)(2,1)}, u32[]{:S(2)}, u32[]{:S(2)}) collective-permute-start(bf16[512,768]{0,1:T(8,128)(2,1)S(1)} %copy-done.6), channel_id=1, source_target_pairs={{0,4},{4,8},{8,12},{12,16},{16,20},{20,24},{24,28},{28,0},{1,5},{5... | collective-permute-start | bytes 2359304 | tf_op jit(solution)/shard_map/while/body/eval_jaxpr/ppermute | solution.py:15
  821.4 32.7 %collective-permute-start.3 = (bf16[512,768]{0,1:T(8,128)(2,1)}, bf16[512,768]{0,1:T(8,128)(2,1)}, u32[]{:S(2)}, u32[]{:S(2)}) collective-permute-start(bf16[512,768]{0,1:T(8,128)(2,1)} %fusion.153), channel_id=1, source_target_pairs={{0,4},{4,8},{8,12},{12,16},{16,20},{20,24},{24,28},{28,0},{1,5},{5... | collective-permute-start | bytes 2359304 | tf_op jit(solution)/shard_map/while/body/eval_jaxpr/ppermute | solution.py:15
  821.4 49.6 %collective-permute-start = (bf16[512,768]{0,1:T(8,128)(2,1)S(1)}, bf16[512,768]{0,1:T(8,128)(2,1)}, u32[]{:S(2)}, u32[]{:S(2)}) collective-permute-start(bf16[512,768]{0,1:T(8,128)(2,1)S(1)} %copy.58), channel_id=1, source_target_pairs={{0,4},{4,8},{8,12},{12,16},{16,20},{20,24},{24,28},{28,0},{1,5},{5... | collective-permute-start | bytes 2359304 | tf_op jit(solution)/shard_map/while/body/eval_jaxpr/ppermute | solution.py:15
  821.4 61.0 %collective-permute-start.1 = (bf16[512,768]{0,1:T(8,128)(2,1)S(1)}, bf16[512,768]{0,1:T(8,128)(2,1)}, u32[]{:S(2)}, u32[]{:S(2)}) collective-permute-start(bf16[512,768]{0,1:T(8,128)(2,1)S(1)} %copy-done.6), channel_id=1, source_target_pairs={{0,4},{4,8},{8,12},{12,16},{16,20},{20,24},{24,28},{28,0},{1,5},{5... | collective-permute-start | bytes 2359304 | tf_op jit(solution)/shard_map/while/body/eval_jaxpr/ppermute | solution.py:15
  904.2 32.7 %collective-permute-start.3 = (bf16[512,768]{0,1:T(8,128)(2,1)}, bf16[512,768]{0,1:T(8,128)(2,1)}, u32[]{:S(2)}, u32[]{:S(2)}) collective-permute-start(bf16[512,768]{0,1:T(8,128)(2,1)} %fusion.153), channel_id=1, source_target_pairs={{0,4},{4,8},{8,12},{12,16},{16,20},{20,24},{24,28},{28,0},{1,5},{5... | collective-permute-start | bytes 2359304 | tf_op jit(solution)/shard_map/while/body/eval_jaxpr/ppermute | solution.py:15
  904.2 49.6 %collective-permute-start = (bf16[512,768]{0,1:T(8,128)(2,1)S(1)}, bf16[512,768]{0,1:T(8,128)(2,1)}, u32[]{:S(2)}, u32[]{:S(2)}) collective-permute-start(bf16[512,768]{0,1:T(8,128)(2,1)S(1)} %copy.58), channel_id=1, source_target_pairs={{0,4},{4,8},{8,12},{12,16},{16,20},{20,24},{24,28},{28,0},{1,5},{5... | collective-permute-start | bytes 2359304 | tf_op jit(solution)/shard_map/while/body/eval_jaxpr/ppermute | solution.py:15
  904.2 60.2 %collective-permute-start.1 = (bf16[512,768]{0,1:T(8,128)(2,1)S(1)}, bf16[512,768]{0,1:T(8,128)(2,1)}, u32[]{:S(2)}, u32[]{:S(2)}) collective-permute-start(bf16[512,768]{0,1:T(8,128)(2,1)S(1)} %copy-done.6), channel_id=1, source_target_pairs={{0,4},{4,8},{8,12},{12,16},{16,20},{20,24},{24,28},{28,0},{1,5},{5... | collective-permute-start | bytes 2359304 | tf_op jit(solution)/shard_map/while/body/eval_jaxpr/ppermute | solution.py:15
  986.1 49.6 %collective-permute-start = (bf16[512,768]{0,1:T(8,128)(2,1)S(1)}, bf16[512,768]{0,1:T(8,128)(2,1)}, u32[]{:S(2)}, u32[]{:S(2)}) collective-permute-start(bf16[512,768]{0,1:T(8,128)(2,1)S(1)} %copy.58), channel_id=1, source_target_pairs={{0,4},{4,8},{8,12},{12,16},{16,20},{20,24},{24,28},{28,0},{1,5},{5... | collective-permute-start | bytes 2359304 | tf_op jit(solution)/shard_map/while/body/eval_jaxpr/ppermute | solution.py:15
  986.1 59.3 %collective-permute-start.1 = (bf16[512,768]{0,1:T(8,128)(2,1)S(1)}, bf16[512,768]{0,1:T(8,128)(2,1)}, u32[]{:S(2)}, u32[]{:S(2)}) collective-permute-start(bf16[512,768]{0,1:T(8,128)(2,1)S(1)} %copy-done.6), channel_id=1, source_target_pairs={{0,4},{4,8},{8,12},{12,16},{16,20},{20,24},{24,28},{28,0},{1,5},{5... | collective-permute-start | bytes 2359304 | tf_op jit(solution)/shard_map/while/body/eval_jaxpr/ppermute | solution.py:15
  1067.2 32.7 %collective-permute-start.3 = (bf16[512,768]{0,1:T(8,128)(2,1)}, bf16[512,768]{0,1:T(8,128)(2,1)}, u32[]{:S(2)}, u32[]{:S(2)}) collective-permute-start(bf16[512,768]{0,1:T(8,128)(2,1)} %fusion.153), channel_id=1, source_target_pairs={{0,4},{4,8},{8,12},{12,16},{16,20},{20,24},{24,28},{28,0},{1,5},{5... | collective-permute-start | bytes 2359304 | tf_op jit(solution)/shard_map/while/body/eval_jaxpr/ppermute | solution.py:15
  1067.2 49.6 %collective-permute-start = (bf16[512,768]{0,1:T(8,128)(2,1)S(1)}, bf16[512,768]{0,1:T(8,128)(2,1)}, u32[]{:S(2)}, u32[]{:S(2)}) collective-permute-start(bf16[512,768]{0,1:T(8,128)(2,1)S(1)} %copy.58), channel_id=1, source_target_pairs={{0,4},{4,8},{8,12},{12,16},{16,20},{20,24},{24,28},{28,0},{1,5},{5... | collective-permute-start | bytes 2359304 | tf_op jit(solution)/shard_map/while/body/eval_jaxpr/ppermute | solution.py:15
  1067.2 58.4 %collective-permute-start.1 = (bf16[512,768]{0,1:T(8,128)(2,1)S(1)}, bf16[512,768]{0,1:T(8,128)(2,1)}, u32[]{:S(2)}, u32[]{:S(2)}) collective-permute-start(bf16[512,768]{0,1:T(8,128)(2,1)S(1)} %copy-done.6), channel_id=1, source_target_pairs={{0,4},{4,8},{8,12},{12,16},{16,20},{20,24},{24,28},{28,0},{1,5},{5... | collective-permute-start | bytes 2359304 | tf_op jit(solution)/shard_map/while/body/eval_jaxpr/ppermute | solution.py:15
  1137.6 154.8 %all-reduce.12.cloned.1.call-start = ((), (), s32[]{:S(2)}) async-start(), calls=%async_computation.14 | async-start | bytes 5013504 | tf_op jit(solution)/shard_map/psum | solution.py:288
  (119 other events, 1920.9 us)
Sparse Core Ops, SparseCore 0:
  9.5 33.4 all-gather.6
  57.5 99.4 all-gather.8
  159.0 97.6 all-gather.10
  258.1 15.6 all-gather.12
  275.2 30.7 all-gather.14
  307.4 20.7 all-gather.16
  446.8 23.7 reduce-scatter.6
  473.8 29.1 reduce-scatter.10
  505.6 40.3 reduce-scatter.8
  1137.8 37.5 reduce-scatter.4
  1179.3 113.0 all-reduce.11
where the time goes:
time: 1310 us; the launch traced here: 1300 us
  waiting for transfers between devices  720 us (55%)
  matrix products  312 us (24%)
  local copies, waits for them, and re-layouts  107 us (8%)
  other arithmetic  102 us (8%)
  blocking collectives  36.8 us (3%)
  between operations  16.7 us (1%)
    ppermute x32, waiting for transfers between devices, passed_along(): return lax.ppermute(x, axis, [(i, (i + by) % count) for i in range(count)])  401 us
    all_gather x1, waiting for transfers between devices, body(): lax.all_gather(keys_local, 'ctx', axis=0, tiled=True)  95.1 us
    all_gather x1, waiting for transfers between devices, body(): lax.all_gather(values_local, 'ctx', axis=0, tiled=True)  87.9 us
    psum x1, waiting for transfers between devices, body(): lax.psum(summed[2].astype(jnp.bfloat16), 'ctx').astype(jnp.float32)  74.8 us
    dot_general x8, matrix products, attend(): jnp.einsum('qhd,khd->hqk', queries, key_part, preferred_element_type=jnp....  59.3 us
    while x152, local copies, waits for them, and re-layouts  56.3 us
    dot_general x8, matrix products, attend(): jnp.einsum('hqk,khd->qhd', weights.astype(jnp.bfloat16), value_part, pref...  50.9 us
    dot_general x8, matrix products, backward_block(): jnp.einsum('hqk,khd->qhd', score_grad, key_part, preferred_element_type=j...  50.8 us
  transfers between devices with their start and end apart: 43, of which 37 were waited for; matrix products, arithmetic and copies ran while one was open for 33% of the time, Pallas kernels for 0%

commit v1 on v0

--- a/solution.py
+++ b/solution.py
@@ -8,6 +8,18 @@
 FF = 1152
 rope_base = 160000.0
 norm_eps = 1e-05
+
+
+def collect(x, axis, dim):
+    ways, here = (lax.axis_size(axis), lax.axis_index(axis))
+    grown, reach = (x, 1)
+    while reach < ways:
+        theirs = lax.ppermute(grown, axis, [(d, d ^ reach) for d in range(ways)])
+        mine_first = jnp.concatenate([grown, theirs], axis=dim)
+        theirs_first = jnp.concatenate([theirs, grown], axis=dim)
+        grown = jnp.where(here & reach == 0, mine_first, theirs_first)
+        reach = 2 * reach
+    return grown
 
 
 def passed_along(x, axis, by):
@@ -128,7 +140,7 @@
     )
     carried = initial
     shards = (
-        lax.all_gather(keys_local, "ctx", axis=0, tiled=True),
+        collect(keys_local, "ctx", 0),
         lax.all_gather(values_local, "ctx", axis=0, tiled=True),
     )
     key_count = shards[0].shape[0]

time: 1310 us -> 1400 us (1.069)
  waiting for transfers between devices: 720 us -> 789 us
  other arithmetic: 102 us -> 129 us
    ppermute x0 -> x3, waiting for transfers between devices: none -> 250 us  [collect(): theirs = lax.ppermute(grown, axis, [(d, d ^ reach) for d in range(ways)])]
    all_gather x1 -> x0, waiting for transfers between devices: 95.1 us -> none  [body(): lax.all_gather(keys_local, 'ctx', axis=0, tiled=True)]
    all_gather x1, waiting for transfers between devices: 87.9 us -> 0.01 us  [body(): lax.all_gather(values_local, 'ctx', axis=0, tiled=True)]
    select_n x0 -> x3, other arithmetic: none -> 14.4 us  [collect(): grown = jnp.where(here & reach == 0, mine_first, theirs_first)]
    unnamed x99 -> x97, local copies, waits for them, and re-layouts: 41.2 us -> 37.7 us
  transfers between devices with their start and end apart: 43 -> 45, of which waited for: 37 -> 38; matrix products, arithmetic and copies ran while one was open for 33% -> 33% of each run, Pallas kernels for 0% -> 0%
where the time goes in v1:
time: 1400 us
  waiting for transfers between devices  789 us (56%)
  matrix products  311 us (22%)
  other arithmetic  129 us (9%)
  local copies, waits for them, and re-layouts  102 us (7%)
  blocking collectives  36.7 us (3%)
  between operations  17.3 us (1%)
    ppermute x32, waiting for transfers between devices, passed_along(): return lax.ppermute(x, axis, [(i, (i + by) % count) for i in range(count)])  405 us
    ppermute x3, waiting for transfers between devices, collect(): theirs = lax.ppermute(grown, axis, [(d, d ^ reach) for d in range(ways)])  250 us
    psum x1, waiting for transfers between devices, body(): lax.psum(summed[2].astype(jnp.bfloat16), 'ctx').astype(jnp.float32)  74.7 us
    dot_general x8, matrix products, attend(): jnp.einsum('qhd,khd->hqk', queries, key_part, preferred_element_type=jnp....  59.4 us
    while x152, local copies, waits for them, and re-layouts  55 us
    dot_general x8, matrix products, backward_block(): jnp.einsum('hqk,khd->qhd', score_grad, key_part, preferred_element_type=j...  50.8 us
    dot_general x8, matrix products, attend(): jnp.einsum('hqk,khd->qhd', weights.astype(jnp.bfloat16), value_part, pref...  50.4 us
    dot_general x8, matrix products, backward_block(): jnp.einsum('hqk,qhd->khd', probs.astype(jnp.bfloat16), grad_rows, preferr...  49.6 us
  transfers between devices with their start and end apart: 45, of which 38 were waited for; matrix products, arithmetic and copies ran while one was open for 33% of the time, Pallas kernels for 0%

profile of v1, /device:TPU:0, one launch (start us, length us, event | category | flops | bytes accessed | tf_op | source)
XLA Modules:
  0.0 1396.2 jit_solution(8143142882791623941)
XLA Ops:
  22.9 20.1 %all-gather.6.cloned.1.call-done = bf16[768,2304]{1,0:T(8,128)(2,1)} async-done(((bf16[192,2304]{1,0:T(8,128)(2,1)}), bf16[768,2304]{1,0:T(8,128)(2,1)}) %all-gather.6.cloned.1.call-update) | async-done | bytes 3538960 | tf_op jit(solution)/shard_map/all_gather | solution.py:100
  65.9 26.8 %collective-permute-done.4 = bf16[512,768]{0,1:T(8,128)(2,1)} collective-permute-done((bf16[512,768]{0,1:T(8,128)(2,1)}, bf16[512,768]{0,1:T(8,128)(2,1)}, u32[]{:S(2)}, u32[]{:S(2)}) %collective-permute-start.4) | collective-permute-done | bytes 786464 | tf_op jit(solution)/shard_map/ppermute | solution.py:17
  96.7 75.9 %collective-permute-done.5 = bf16[1024,768]{0,1:T(8,128)(2,1)} collective-permute-done((bf16[1024,768]{0,1:T(8,128)(2,1)S(1)}, bf16[1024,768]{0,1:T(8,128)(2,1)}, u32[]{:S(2)}, u32[]{:S(2)}) %collective-permute-start.5) | collective-permute-done | bytes 1572896 | tf_op jit(solution)/shard_map/ppermute | solution.py:17
  177.4 147.2 %collective-permute-done.6 = bf16[2048,768]{0,1:T(8,128)(2,1)} collective-permute-done((bf16[2048,768]{0,1:T(8,128)(2,1)}, bf16[2048,768]{0,1:T(8,128)(2,1)}, u32[]{:S(2)}, u32[]{:S(2)}) %collective-permute-start.6) | collective-permute-done | bytes 3145760 | tf_op jit(solution)/shard_map/ppermute | solution.py:17
  353.7 143.8 %while.40 = (s32[]{:T(128)}, f32[12,512]{1,0:T(8,128)S(1)}, f32[12,512]{1,0:T(8,128)S(1)}, f32[512,12,64]{0,2,1:T(8,128)S(1)}, bf16[8,512,12,64]{1,3,2,0:T(8,128...) while((s32[]{:T(128)}, f32[12,512]{1,0:T(8,128)S(1)}, ...), condition=%wide.region_5.6_spmd.clone, body=%wide.region_2.5_spmd.clone.sunk | while | flops 831688704 | bytes 93979776 | solution.py:150
  543.2 673.9 %while.41 = (s32[]{:T(128)}, bf16[512,768]{0,1:T(8,128)(2,1)}, bf16[512,768]{0,1:T(8,128)(2,1)}, f32[512,768]{0,1:T(8,128)}, f32[512,768]{0,1:T(8,128)}, /*index...) while((s32[]{:T(128)}, bf16[512,768]{0,1:T(8,128)(2,1)}, ...), condition=%wide.region_12.13_spmd.clone, body=%wide.region_11.12_spmd.clone.sunk | while | flops 2043150336 | bytes 191177200 | solution.py:265
  582.1 14.4 %collective-permute-done.3 = bf16[512,768]{0,1:T(8,128)(2,1)} collective-permute-done((bf16[512,768]{0,1:T(8,128)(2,1)}, bf16[512,768]{0,1:T(8,128)(2,1)}, u32[]{:S(2)}, u32[]{:S(2)}) %collective-permute-start.3) | collective-permute-done | bytes 786464 | tf_op jit(solution)/shard_map/while/body/eval_jaxpr/ppermute | solution.py:27
  599.0 14.3 %collective-permute-done = bf16[512,768]{0,1:T(8,128)(2,1)} collective-permute-done((bf16[512,768]{0,1:T(8,128)(2,1)S(1)}, bf16[512,768]{0,1:T(8,128)(2,1)}, u32[]{:S(2)}, u32[]{:S(2)}) %collective-permute-start) | collective-permute-done | bytes 786464 | tf_op jit(solution)/shard_map/while/body/eval_jaxpr/ppermute | solution.py:27
  613.3 16.0 %collective-permute-done.1 = bf16[512,768]{0,1:T(8,128)(2,1)} collective-permute-done((bf16[512,768]{0,1:T(8,128)(2,1)S(1)}, bf16[512,768]{0,1:T(8,128)(2,1)}, u32[]{:S(2)}, u32[]{:S(2)}) %collective-permute-start.1) | collective-permute-done | bytes 786464 | tf_op jit(solution)/shard_map/while/body/eval_jaxpr/ppermute | solution.py:27
  669.5 14.4 %collective-permute-done.3 = bf16[512,768]{0,1:T(8,128)(2,1)} collective-permute-done((bf16[512,768]{0,1:T(8,128)(2,1)}, bf16[512,768]{0,1:T(8,128)(2,1)}, u32[]{:S(2)}, u32[]{:S(2)}) %collective-permute-start.3) | collective-permute-done | bytes 786464 | tf_op jit(solution)/shard_map/while/body/eval_jaxpr/ppermute | solution.py:27
  686.4 14.4 %collective-permute-done = bf16[512,768]{0,1:T(8,128)(2,1)} collective-permute-done((bf16[512,768]{0,1:T(8,128)(2,1)S(1)}, bf16[512,768]{0,1:T(8,128)(2,1)}, u32[]{:S(2)}, u32[]{:S(2)}) %collective-permute-start) | collective-permute-done | bytes 786464 | tf_op jit(solution)/shard_map/while/body/eval_jaxpr/ppermute | solution.py:27
  700.7 15.2 %collective-permute-done.1 = bf16[512,768]{0,1:T(8,128)(2,1)} collective-permute-done((bf16[512,768]{0,1:T(8,128)(2,1)S(1)}, bf16[512,768]{0,1:T(8,128)(2,1)}, u32[]{:S(2)}, u32[]{:S(2)}) %collective-permute-start.1) | collective-permute-done | bytes 786464 | tf_op jit(solution)/shard_map/while/body/eval_jaxpr/ppermute | solution.py:27
  756.0 14.4 %collective-permute-done.3 = bf16[512,768]{0,1:T(8,128)(2,1)} collective-permute-done((bf16[512,768]{0,1:T(8,128)(2,1)}, bf16[512,768]{0,1:T(8,128)(2,1)}, u32[]{:S(2)}, u32[]{:S(2)}) %collective-permute-start.3) | collective-permute-done | bytes 786464 | tf_op jit(solution)/shard_map/while/body/eval_jaxpr/ppermute | solution.py:27
  772.9 14.4 %collective-permute-done = bf16[512,768]{0,1:T(8,128)(2,1)} collective-permute-done((bf16[512,768]{0,1:T(8,128)(2,1)S(1)}, bf16[512,768]{0,1:T(8,128)(2,1)}, u32[]{:S(2)}, u32[]{:S(2)}) %collective-permute-start) | collective-permute-done | bytes 786464 | tf_op jit(solution)/shard_map/while/body/eval_jaxpr/ppermute | solution.py:27
  787.3 14.3 %collective-permute-done.1 = bf16[512,768]{0,1:T(8,128)(2,1)} collective-permute-done((bf16[512,768]{0,1:T(8,128)(2,1)S(1)}, bf16[512,768]{0,1:T(8,128)(2,1)}, u32[]{:S(2)}, u32[]{:S(2)}) %collective-permute-start.1) | collective-permute-done | bytes 786464 | tf_op jit(solution)/shard_map/while/body/eval_jaxpr/ppermute | solution.py:27
  841.7 14.4 %collective-permute-done.3 = bf16[512,768]{0,1:T(8,128)(2,1)} collective-permute-done((bf16[512,768]{0,1:T(8,128)(2,1)}, bf16[512,768]{0,1:T(8,128)(2,1)}, u32[]{:S(2)}, u32[]{:S(2)}) %collective-permute-start.3) | collective-permute-done | bytes 786464 | tf_op jit(solution)/shard_map/while/body/eval_jaxpr/ppermute | solution.py:27
  858.6 14.4 %collective-permute-done = bf16[512,768]{0,1:T(8,128)(2,1)} collective-permute-done((bf16[512,768]{0,1:T(8,128)(2,1)S(1)}, bf16[512,768]{0,1:T(8,128)(2,1)}, u32[]{:S(2)}, u32[]{:S(2)}) %collective-permute-start) | collective-permute-done | bytes 786464 | tf_op jit(solution)/shard_map/while/body/eval_jaxpr/ppermute | solution.py:27
  872.9 13.5 collective-permute-done.1
  926.5 14.4 %collective-permute-done.3 = bf16[512,768]{0,1:T(8,128)(2,1)} collective-permute-done((bf16[512,768]{0,1:T(8,128)(2,1)}, bf16[512,768]{0,1:T(8,128)(2,1)}, u32[]{:S(2)}, u32[]{:S(2)}) %collective-permute-start.3) | collective-permute-done | bytes 786464 | tf_op jit(solution)/shard_map/while/body/eval_jaxpr/ppermute | solution.py:27
  943.4 14.4 %collective-permute-done = bf16[512,768]{0,1:T(8,128)(2,1)} collective-permute-done((bf16[512,768]{0,1:T(8,128)(2,1)S(1)}, bf16[512,768]{0,1:T(8,128)(2,1)}, u32[]{:S(2)}, u32[]{:S(2)}) %collective-permute-start) | collective-permute-done | bytes 786464 | tf_op jit(solution)/shard_map/while/body/eval_jaxpr/ppermute | solution.py:27
  957.7 12.6 collective-permute-done.1
  1010.5 14.4 %collective-permute-done.3 = bf16[512,768]{0,1:T(8,128)(2,1)} collective-permute-done((bf16[512,768]{0,1:T(8,128)(2,1)}, bf16[512,768]{0,1:T(8,128)(2,1)}, u32[]{:S(2)}, u32[]{:S(2)}) %collective-permute-start.3) | collective-permute-done | bytes 786464 | tf_op jit(solution)/shard_map/while/body/eval_jaxpr/ppermute | solution.py:27
  1027.3 14.4 %collective-permute-done = bf16[512,768]{0,1:T(8,128)(2,1)} collective-permute-done((bf16[512,768]{0,1:T(8,128)(2,1)S(1)}, bf16[512,768]{0,1:T(8,128)(2,1)}, u32[]{:S(2)}, u32[]{:S(2)}) %collective-permute-start) | collective-permute-done | bytes 786464 | tf_op jit(solution)/shard_map/while/body/eval_jaxpr/ppermute | solution.py:27
  1041.7 11.8 collective-permute-done.1
  1093.6 14.4 %collective-permute-done.3 = bf16[512,768]{0,1:T(8,128)(2,1)} collective-permute-done((bf16[512,768]{0,1:T(8,128)(2,1)}, bf16[512,768]{0,1:T(8,128)(2,1)}, u32[]{:S(2)}, u32[]{:S(2)}) %collective-permute-start.3) | collective-permute-done | bytes 786464 | tf_op jit(solution)/shard_map/while/body/eval_jaxpr/ppermute | solution.py:27
  1110.4 14.4 %collective-permute-done = bf16[512,768]{0,1:T(8,128)(2,1)} collective-permute-done((bf16[512,768]{0,1:T(8,128)(2,1)S(1)}, bf16[512,768]{0,1:T(8,128)(2,1)}, u32[]{:S(2)}, u32[]{:S(2)}) %collective-permute-start) | collective-permute-done | bytes 786464 | tf_op jit(solution)/shard_map/while/body/eval_jaxpr/ppermute | solution.py:27
  1124.8 10.9 collective-permute-done.1
  1175.8 14.4 %collective-permute-done.3 = bf16[512,768]{0,1:T(8,128)(2,1)} collective-permute-done((bf16[512,768]{0,1:T(8,128)(2,1)}, bf16[512,768]{0,1:T(8,128)(2,1)}, u32[]{:S(2)}, u32[]{:S(2)}) %collective-permute-start.3) | collective-permute-done | bytes 786464 | tf_op jit(solution)/shard_map/while/body/eval_jaxpr/ppermute | solution.py:27
  1192.7 14.4 %collective-permute-done = bf16[512,768]{0,1:T(8,128)(2,1)} collective-permute-done((bf16[512,768]{0,1:T(8,128)(2,1)S(1)}, bf16[512,768]{0,1:T(8,128)(2,1)}, u32[]{:S(2)}, u32[]{:S(2)}) %collective-permute-start) | collective-permute-done | bytes 786464 | tf_op jit(solution)/shard_map/while/body/eval_jaxpr/ppermute | solution.py:27
  1228.7 37.6 %reduce-scatter.5.cloned.1.call-done = bf16[192,2304]{1,0:T(8,128)(2,1)} async-done(((bf16[768,2304]{1,0:T(8,128)(2,1)}), bf16[192,2304]{1,0:T(8,128)(2,1)}) %reduce-scatter.5.cloned.1.call-update) | async-done | bytes 884752 | tf_op jit(solution)/shard_map/reduce_scatter | solution.py:284
  1279.1 22.6 %all-reduce.6 = (bf16[192]{0:T(256)(128)(2,1)S(1)}, bf16[192]{0:T(256)(128)(2,1)S(1)}) all-reduce(bf16[192]{0:T(256)(128)(2,1)S(1)} %dynamic-slice.3, bf16[192]{0:T(256)(128)(2,1)S(1)} %dynamic-slice.5), channel_id=1, replica_groups=mesh['ctx'=8,'dp'=4] {'ctx'}, use_global_device_ids=true, to_apply=%region_17.18 | all-reduce | flops 384 | bytes 1536 | tf_op jit(solution)/shard_map/psum | solution.py:298
  1308.4 74.7 %all-reduce.12.cloned.1.call-done = (bf16[192,2304]{1,0:T(8,128)(2,1)}, bf16[192,768]{1,0:T(8,128)(2,1)}, bf16[192,2304]{1,0:T(8,128)(2,1)}, bf16[288,768]{1,0:T(8,128)(2,1)}) async-done(((bf16[192,2304]{1,0:T(8,128)(2,1)}, bf16[192,768]{1,0:T(8,128)(2,1)}, bf16[192,2304]{1,0:T(8,128)(2,1)}, bf16[288,768]{1,0:T(8,128)(2,1)}), (bf16[192,2304]{1,0:T(8,128)(2,1)}, bf16[192,768]{1,0:T(8,128)(2,1)}, ...) | async-done | bytes 2506768 | tf_op jit(solution)/shard_map/psum | solution.py:300
  (501 shorter events, 648.7 us)
Async XLA Ops:
  7.2 35.9 %all-gather.6.cloned.1.call-start = ((), (), s32[]{:S(2)}) async-start(), calls=%async_computation.4 | async-start | bytes 4423680 | tf_op jit(solution)/shard_map/all_gather | solution.py:100
  7.9 333.5 %all-gather.8.cloned.1.call-start = ((), (), s32[]{:S(2)}) async-start(), calls=%async_computation.5 | async-start | bytes 7077888 | tf_op jit(solution)/shard_map/all_gather | solution.py:144
  56.3 442.5 %all-gather.10.cloned.1.call-start = ((), (), s32[]{:S(2)}) async-start(), calls=%async_computation.6 | async-start | bytes 1474560 | tf_op jit(solution)/shard_map/all_gather | solution.py:101
  57.1 445.7 %all-gather.12.cloned.1.call-start = ((), (), s32[]{:S(2)}) async-start(), calls=%async_computation.7 | async-start | bytes 4423680 | tf_op jit(solution)/shard_map/all_gather | solution.py:102
  65.9 443.7 %all-gather.14.cloned.1.call-start = ((), (), s32[]{:S(2)}) async-start(), calls=%async_computation.8 | async-start | bytes 2211840 | tf_op jit(solution)/shard_map/all_gather | solution.py:103
  95.2 77.4 %collective-permute-start.5 = (bf16[1024,768]{0,1:T(8,128)(2,1)S(1)}, bf16[1024,768]{0,1:T(8,128)(2,1)}, u32[]{:S(2)}, u32[]{:S(2)}) collective-permute-start(bf16[1024,768]{0,1:T(8,128)(2,1)S(1)} %maximum_select_fusion.2), channel_id=1, source_target_pairs={{0,8},{4,12},{8,0},{12,4},{16,24},{20,28},{24,16},{28,20},{1,9},{5... | collective-permute-start | bytes 4718600 | tf_op jit(solution)/shard_map/ppermute | solution.py:17
  176.8 147.7 %collective-permute-start.6 = (bf16[2048,768]{0,1:T(8,128)(2,1)}, bf16[2048,768]{0,1:T(8,128)(2,1)}, u32[]{:S(2)}, u32[]{:S(2)}) collective-permute-start(bf16[2048,768]{0,1:T(8,128)(2,1)} %maximum_select_fusion.1), channel_id=1, source_target_pairs={{0,16},{4,20},{8,24},{12,28},{16,0},{20,4},{24,8},{28,12},{1,17},{... | collective-permute-start | bytes 9437192 | tf_op jit(solution)/shard_map/ppermute | solution.py:17
  177.3 1051.4 %reduce-scatter.7.cloned.1.call-start = ((), (), s32[]{:S(2)}) async-start(), calls=%async_computation.10 | async-start | bytes 1474560 | tf_op jit(solution)/shard_map/reduce_scatter | solution.py:287
  529.6 699.1 %reduce-scatter.11.cloned.1.call-start = ((), (), s32[]{:S(2)}) async-start(), calls=%async_computation.12 | async-start | bytes 2211840 | tf_op jit(solution)/shard_map/reduce_scatter | solution.py:293
  532.0 696.7 %reduce-scatter.9.cloned.1.call-start = ((), (), s32[]{:S(2)}) async-start(), calls=%async_computation.11 | async-start | bytes 4423680 | tf_op jit(solution)/shard_map/reduce_scatter | solution.py:290
  543.1 723.2 %reduce-scatter.5.cloned.1.call-start = ((), (), s32[]{:S(2)}) async-start(), calls=%async_computation.9 | async-start | bytes 4423680 | tf_op jit(solution)/shard_map/reduce_scatter | solution.py:284
  563.8 32.7 %collective-permute-start.3 = (bf16[512,768]{0,1:T(8,128)(2,1)}, bf16[512,768]{0,1:T(8,128)(2,1)}, u32[]{:S(2)}, u32[]{:S(2)}) collective-permute-start(bf16[512,768]{0,1:T(8,128)(2,1)} %fusion.153), channel_id=1, source_target_pairs={{0,4},{4,8},{8,12},{12,16},{16,20},{20,24},{24,28},{28,0},{1,5},{5... | collective-permute-start | bytes 2359304 | tf_op jit(solution)/shard_map/while/body/eval_jaxpr/ppermute | solution.py:27
  563.8 49.6 %collective-permute-start = (bf16[512,768]{0,1:T(8,128)(2,1)S(1)}, bf16[512,768]{0,1:T(8,128)(2,1)}, u32[]{:S(2)}, u32[]{:S(2)}) collective-permute-start(bf16[512,768]{0,1:T(8,128)(2,1)S(1)} %copy.58), channel_id=1, source_target_pairs={{0,4},{4,8},{8,12},{12,16},{16,20},{20,24},{24,28},{28,0},{1,5},{5... | collective-permute-start | bytes 2359304 | tf_op jit(solution)/shard_map/while/body/eval_jaxpr/ppermute | solution.py:27
  563.8 65.6 %collective-permute-start.1 = (bf16[512,768]{0,1:T(8,128)(2,1)S(1)}, bf16[512,768]{0,1:T(8,128)(2,1)}, u32[]{:S(2)}, u32[]{:S(2)}) collective-permute-start(bf16[512,768]{0,1:T(8,128)(2,1)S(1)} %copy-done.6), channel_id=1, source_target_pairs={{0,4},{4,8},{8,12},{12,16},{16,20},{20,24},{24,28},{28,0},{1,5},{5... | collective-permute-start | bytes 2359304 | tf_op jit(solution)/shard_map/while/body/eval_jaxpr/ppermute | solution.py:27
  651.2 32.7 %collective-permute-start.3 = (bf16[512,768]{0,1:T(8,128)(2,1)}, bf16[512,768]{0,1:T(8,128)(2,1)}, u32[]{:S(2)}, u32[]{:S(2)}) collective-permute-start(bf16[512,768]{0,1:T(8,128)(2,1)} %fusion.153), channel_id=1, source_target_pairs={{0,4},{4,8},{8,12},{12,16},{16,20},{20,24},{24,28},{28,0},{1,5},{5... | collective-permute-start | bytes 2359304 | tf_op jit(solution)/shard_map/while/body/eval_jaxpr/ppermute | solution.py:27
  651.2 49.6 %collective-permute-start = (bf16[512,768]{0,1:T(8,128)(2,1)S(1)}, bf16[512,768]{0,1:T(8,128)(2,1)}, u32[]{:S(2)}, u32[]{:S(2)}) collective-permute-start(bf16[512,768]{0,1:T(8,128)(2,1)S(1)} %copy.58), channel_id=1, source_target_pairs={{0,4},{4,8},{8,12},{12,16},{16,20},{20,24},{24,28},{28,0},{1,5},{5... | collective-permute-start | bytes 2359304 | tf_op jit(solution)/shard_map/while/body/eval_jaxpr/ppermute | solution.py:27
  651.2 64.7 %collective-permute-start.1 = (bf16[512,768]{0,1:T(8,128)(2,1)S(1)}, bf16[512,768]{0,1:T(8,128)(2,1)}, u32[]{:S(2)}, u32[]{:S(2)}) collective-permute-start(bf16[512,768]{0,1:T(8,128)(2,1)S(1)} %copy-done.6), channel_id=1, source_target_pairs={{0,4},{4,8},{8,12},{12,16},{16,20},{20,24},{24,28},{28,0},{1,5},{5... | collective-permute-start | bytes 2359304 | tf_op jit(solution)/shard_map/while/body/eval_jaxpr/ppermute | solution.py:27
  737.7 32.7 %collective-permute-start.3 = (bf16[512,768]{0,1:T(8,128)(2,1)}, bf16[512,768]{0,1:T(8,128)(2,1)}, u32[]{:S(2)}, u32[]{:S(2)}) collective-permute-start(bf16[512,768]{0,1:T(8,128)(2,1)} %fusion.153), channel_id=1, source_target_pairs={{0,4},{4,8},{8,12},{12,16},{16,20},{20,24},{24,28},{28,0},{1,5},{5... | collective-permute-start | bytes 2359304 | tf_op jit(solution)/shard_map/while/body/eval_jaxpr/ppermute | solution.py:27
  737.7 49.6 %collective-permute-start = (bf16[512,768]{0,1:T(8,128)(2,1)S(1)}, bf16[512,768]{0,1:T(8,128)(2,1)}, u32[]{:S(2)}, u32[]{:S(2)}) collective-permute-start(bf16[512,768]{0,1:T(8,128)(2,1)S(1)} %copy.58), channel_id=1, source_target_pairs={{0,4},{4,8},{8,12},{12,16},{16,20},{20,24},{24,28},{28,0},{1,5},{5... | collective-permute-start | bytes 2359304 | tf_op jit(solution)/shard_map/while/body/eval_jaxpr/ppermute | solution.py:27
  737.7 63.9 %collective-permute-start.1 = (bf16[512,768]{0,1:T(8,128)(2,1)S(1)}, bf16[512,768]{0,1:T(8,128)(2,1)}, u32[]{:S(2)}, u32[]{:S(2)}) collective-permute-start(bf16[512,768]{0,1:T(8,128)(2,1)S(1)} %copy-done.6), channel_id=1, source_target_pairs={{0,4},{4,8},{8,12},{12,16},{16,20},{20,24},{24,28},{28,0},{1,5},{5... | collective-permute-start | bytes 2359304 | tf_op jit(solution)/shard_map/while/body/eval_jaxpr/ppermute | solution.py:27
  823.4 49.6 %collective-permute-start = (bf16[512,768]{0,1:T(8,128)(2,1)S(1)}, bf16[512,768]{0,1:T(8,128)(2,1)}, u32[]{:S(2)}, u32[]{:S(2)}) collective-permute-start(bf16[512,768]{0,1:T(8,128)(2,1)S(1)} %copy.58), channel_id=1, source_target_pairs={{0,4},{4,8},{8,12},{12,16},{16,20},{20,24},{24,28},{28,0},{1,5},{5... | collective-permute-start | bytes 2359304 | tf_op jit(solution)/shard_map/while/body/eval_jaxpr/ppermute | solution.py:27
  823.4 63.0 %collective-permute-start.1 = (bf16[512,768]{0,1:T(8,128)(2,1)S(1)}, bf16[512,768]{0,1:T(8,128)(2,1)}, u32[]{:S(2)}, u32[]{:S(2)}) collective-permute-start(bf16[512,768]{0,1:T(8,128)(2,1)S(1)} %copy-done.6), channel_id=1, source_target_pairs={{0,4},{4,8},{8,12},{12,16},{16,20},{20,24},{24,28},{28,0},{1,5},{5... | collective-permute-start | bytes 2359304 | tf_op jit(solution)/shard_map/while/body/eval_jaxpr/ppermute | solution.py:27
  908.2 49.6 %collective-permute-start = (bf16[512,768]{0,1:T(8,128)(2,1)S(1)}, bf16[512,768]{0,1:T(8,128)(2,1)}, u32[]{:S(2)}, u32[]{:S(2)}) collective-permute-start(bf16[512,768]{0,1:T(8,128)(2,1)S(1)} %copy.58), channel_id=1, source_target_pairs={{0,4},{4,8},{8,12},{12,16},{16,20},{20,24},{24,28},{28,0},{1,5},{5... | collective-permute-start | bytes 2359304 | tf_op jit(solution)/shard_map/while/body/eval_jaxpr/ppermute | solution.py:27
  908.2 62.2 %collective-permute-start.1 = (bf16[512,768]{0,1:T(8,128)(2,1)S(1)}, bf16[512,768]{0,1:T(8,128)(2,1)}, u32[]{:S(2)}, u32[]{:S(2)}) collective-permute-start(bf16[512,768]{0,1:T(8,128)(2,1)S(1)} %copy-done.6), channel_id=1, source_target_pairs={{0,4},{4,8},{8,12},{12,16},{16,20},{20,24},{24,28},{28,0},{1,5},{5... | collective-permute-start | bytes 2359304 | tf_op jit(solution)/shard_map/while/body/eval_jaxpr/ppermute | solution.py:27
  992.1 49.6 %collective-permute-start = (bf16[512,768]{0,1:T(8,128)(2,1)S(1)}, bf16[512,768]{0,1:T(8,128)(2,1)}, u32[]{:S(2)}, u32[]{:S(2)}) collective-permute-start(bf16[512,768]{0,1:T(8,128)(2,1)S(1)} %copy.58), channel_id=1, source_target_pairs={{0,4},{4,8},{8,12},{12,16},{16,20},{20,24},{24,28},{28,0},{1,5},{5... | collective-permute-start | bytes 2359304 | tf_op jit(solution)/shard_map/while/body/eval_jaxpr/ppermute | solution.py:27
  992.1 61.3 %collective-permute-start.1 = (bf16[512,768]{0,1:T(8,128)(2,1)S(1)}, bf16[512,768]{0,1:T(8,128)(2,1)}, u32[]{:S(2)}, u32[]{:S(2)}) collective-permute-start(bf16[512,768]{0,1:T(8,128)(2,1)S(1)} %copy-done.6), channel_id=1, source_target_pairs={{0,4},{4,8},{8,12},{12,16},{16,20},{20,24},{24,28},{28,0},{1,5},{5... | collective-permute-start | bytes 2359304 | tf_op jit(solution)/shard_map/while/body/eval_jaxpr/ppermute | solution.py:27
  1075.2 32.7 %collective-permute-start.3 = (bf16[512,768]{0,1:T(8,128)(2,1)}, bf16[512,768]{0,1:T(8,128)(2,1)}, u32[]{:S(2)}, u32[]{:S(2)}) collective-permute-start(bf16[512,768]{0,1:T(8,128)(2,1)} %fusion.153), channel_id=1, source_target_pairs={{0,4},{4,8},{8,12},{12,16},{16,20},{20,24},{24,28},{28,0},{1,5},{5... | collective-permute-start | bytes 2359304 | tf_op jit(solution)/shard_map/while/body/eval_jaxpr/ppermute | solution.py:27
  1075.2 49.6 %collective-permute-start = (bf16[512,768]{0,1:T(8,128)(2,1)S(1)}, bf16[512,768]{0,1:T(8,128)(2,1)}, u32[]{:S(2)}, u32[]{:S(2)}) collective-permute-start(bf16[512,768]{0,1:T(8,128)(2,1)S(1)} %copy.58), channel_id=1, source_target_pairs={{0,4},{4,8},{8,12},{12,16},{16,20},{20,24},{24,28},{28,0},{1,5},{5... | collective-permute-start | bytes 2359304 | tf_op jit(solution)/shard_map/while/body/eval_jaxpr/ppermute | solution.py:27
  1075.2 60.5 %collective-permute-start.1 = (bf16[512,768]{0,1:T(8,128)(2,1)S(1)}, bf16[512,768]{0,1:T(8,128)(2,1)}, u32[]{:S(2)}, u32[]{:S(2)}) collective-permute-start(bf16[512,768]{0,1:T(8,128)(2,1)S(1)} %copy-done.6), channel_id=1, source_target_pairs={{0,4},{4,8},{8,12},{12,16},{16,20},{20,24},{24,28},{28,0},{1,5},{5... | collective-permute-start | bytes 2359304 | tf_op jit(solution)/shard_map/while/body/eval_jaxpr/ppermute | solution.py:27
  1157.5 49.6 %collective-permute-start = (bf16[512,768]{0,1:T(8,128)(2,1)S(1)}, bf16[512,768]{0,1:T(8,128)(2,1)}, u32[]{:S(2)}, u32[]{:S(2)}) collective-permute-start(bf16[512,768]{0,1:T(8,128)(2,1)S(1)} %copy.58), channel_id=1, source_target_pairs={{0,4},{4,8},{8,12},{12,16},{16,20},{20,24},{24,28},{28,0},{1,5},{5... | collective-permute-start | bytes 2359304 | tf_op jit(solution)/shard_map/while/body/eval_jaxpr/ppermute | solution.py:27
  1157.5 59.6 %collective-permute-start.1 = (bf16[512,768]{0,1:T(8,128)(2,1)S(1)}, bf16[512,768]{0,1:T(8,128)(2,1)}, u32[]{:S(2)}, u32[]{:S(2)}) collective-permute-start(bf16[512,768]{0,1:T(8,128)(2,1)S(1)} %copy-done.6), channel_id=1, source_target_pairs={{0,4},{4,8},{8,12},{12,16},{16,20},{20,24},{24,28},{28,0},{1,5},{5... | collective-permute-start | bytes 2359304 | tf_op jit(solution)/shard_map/while/body/eval_jaxpr/ppermute | solution.py:27
  1228.3 154.8 %all-reduce.12.cloned.1.call-start = ((), (), s32[]{:S(2)}) async-start(), calls=%async_computation.13 | async-start | bytes 5013504 | tf_op jit(solution)/shard_map/psum | solution.py:300
  (120 other events, 2010.7 us)
Sparse Core Ops, SparseCore 0:
  9.5 33.4 all-gather.5
  56.4 209.0 all-gather.7
  267.1 14.9 all-gather.9
  283.5 30.7 all-gather.11
  315.7 20.7 all-gather.13
  529.7 23.0 reduce-scatter.6
  556.0 29.1 reduce-scatter.10
  587.8 40.3 reduce-scatter.8
  1228.5 37.7 reduce-scatter.4
  1270.0 113.0 all-reduce.11
